TPU v7x, 128 devices: a whole 4x4x4 slice. The times are simulated.
128 devices in a mesh: layer: 16 (over z_lo, x, core), lat: 8 (over z_hi, y).
Axes of the slice: x: 4, y: 4, z: 4 (z_hi: 2, z_lo: 2; z = z_hi * 2 + z_lo), core: 2. Of those that a mesh axis runs over, the one named last changes fastest.
Arguments:
- saved_codes: bfloat16 [16, 512, 1024], P('layer', 'lat'), may hold values from 0.049804688 to 2
- relu_mask: int32 [16, 512, 1024], P('layer', 'lat'), may hold values 0 or 1
- errors: bfloat16 [16, 1024, 4096], P('layer'), may hold values from -0.29882812 to 0.29882812
- decoders: bfloat16 [16, 16, 512, 4096], P('layer', None, 'lat'), may hold values from -0.59765625 to 0.59765625
- inputs: bfloat16 [16, 1024, 4096], P('layer'), may hold values from -0.3984375 to 0.3984375
Outputs:
- decoder_grad: bfloat16 [16, 16, 512, 4096], P('layer', None, 'lat')
- code_grad: float32 [16, 512, 1024], P('layer', 'lat')
- encoder_grad: bfloat16 [16, 512, 4096], P('layer', 'lat')
All inputs are finite; a program needn't handle non-finite values. No bound on the sum of `relu_mask` on one device may be relied on, other than what follows from the above.
Results may differ from a plain program's by a relative error of at most 0.0049.
Values may be sent and summed in bfloat16 or wider, within the bound.
No kernel may reach another device: no remote copies, remote signals or barrier semaphores. Data moves between devices by JAX's collectives and lax.ppermute only.
A program may use at most 128 MiB of HBM per device.

v0:
```python
import jax
import jax.numpy as jnp
from jax import lax
from jax.sharding import PartitionSpec as P


def body(saved_codes, relu_mask, errors, decoders, inputs):
    target = lax.axis_index("layer")
    target_error = errors[0]
    latents = saved_codes.shape[1]
    tokens = saved_codes.shape[2]
    model_width = target_error.shape[1]
    active = saved_codes * relu_mask.astype(jnp.bfloat16)
    gathered = lax.all_gather(active, "layer", axis=0, tiled=True)
    row_count = gathered.shape[0]
    allowed = (jnp.arange(row_count, dtype=jnp.int32) <= target)[:, None, None]

    def decoder_compute():
        products = jnp.dot(
            gathered.reshape(row_count * latents, tokens),
            target_error,
            preferred_element_type=jnp.float32,
        )
        products = products.reshape(row_count, latents, model_width)
        return jnp.where(allowed, products, 0.0).astype(jnp.bfloat16)

    def decoder_skipped():
        return jnp.zeros((row_count, latents, model_width), jnp.bfloat16)

    decoder_grad = lax.cond(jnp.int32(0) <= target, decoder_compute, decoder_skipped)
    code_row_count = 1 * lax.axis_size("layer")
    code_allowed = (jnp.arange(code_row_count, dtype=jnp.int32) <= target)[:, None, None]

    def code_compute():
        slab_rows = decoders[0]
        products = lax.dot_general(
            slab_rows.reshape(code_row_count * latents, model_width),
            target_error,
            (((1,), (1,)), ((), ())),
            preferred_element_type=jnp.float32,
        )
        products = products.reshape(code_row_count, latents, tokens)
        return jnp.where(code_allowed, products, 0.0)

    def code_skipped():
        return jnp.zeros((code_row_count, latents, tokens), jnp.float32)

    code_grad = lax.psum_scatter(
        lax.cond(jnp.int32(0) <= target, code_compute, code_skipped),
        "layer",
        scatter_dimension=0,
        tiled=True,
    )
    pre_grad = (code_grad[0] * relu_mask[0].astype(jnp.float32)).astype(jnp.bfloat16)
    encoder_grad = jnp.dot(pre_grad, inputs[0], preferred_element_type=jnp.float32).astype(
        jnp.bfloat16
    )
    return (decoder_grad[None], code_grad, encoder_grad[None])


def solution(mesh):
    return jax.shard_map(
        body,
        mesh=mesh,
        in_specs=(
            P("layer", "lat", None),
            P("layer", "lat", None),
            P("layer", None, None),
            P("layer", None, "lat", None),
            P("layer", None, None),
        ),
        out_specs=(P("layer", None, "lat", None), P("layer", "lat", None), P("layer", "lat", None)),
        check_vma=False,
    )
```

profile of v0, /device:TPU:0, one launch (start us, length us, event | category | flops | bytes accessed | tf_op | source)
XLA Modules:
  0.0 129.6 jit_solution(15806542635642984849)
XLA Ops:
  7.2 0.0 all-gather.2.cloned.1.call-start
  7.2 1.7 %convert_multiply_fusion = bf16[1,64,1024]{2,1,0:T(8,128)(2,1)} fusion(bf16[1,64,1024]{2,1,0:T(8,128)(2,1)} %param.9, s32[1,64,1024]{2,1,0:T(8,128)} %param.10), kind=kLoop, calls=%fused_computation.14 | loop fusion | flops 131072 | bytes 524288 | tf_op jit(solution)/shard_map/mul | solution.py:13
  8.9 0.0 all-gather.2.cloned.1.call-update
  8.9 0.0 reduce-scatter.2.cloned.1.call-start
  9.0 15.1 %conditional.3 = (f32[16,64,1024]{2,1,0:T(8,128)}) conditional(s32[]{:T(128)} %convert_element_type.23, () %tuple.24, (pred[16,1,1]{0,2,1:T(4,128)(4,1)S(1)}, bf16[1,16,64,4096]{3,2,1,0:T(8,128)(2,1)}, bf16[1024,4096]{1,0:T(8,128)(2,1)}) %tuple.35), branch_computations={%region_2.3_spmd, %region_3.4_spmd} | conditional | flops 8590983168 | bytes 20971544 | solution.py:49
  9.0 15.1 %broadcast_select_fusion = f32[16,64,1024]{2,1,0:T(8,128)} fusion(pred[16]{0:T(512)(128)(4,1)S(1)} %bitcast.35, bf16[1024,4096]{1,0:T(8,128)(2,1)} %get-tuple-element.24, bf16[1,16,64,4096]{3,2,1,0:T(8,128)(2,1)} %get-tuple-element.29), kind=kOutput, calls=%fused_computation.7 | convolution fusion | flops 8590983168 | bytes 20971536 | tf_op jit(solution)/shard_map/cond/branch_1_fun/dot_general | solution.py:36
  24.1 0.0 reduce-scatter.2.cloned.1.call-update
  24.1 22.5 %all-gather.2.cloned.1.call-done = bf16[16,64,1024]{2,1,0:T(8,128)(2,1)} async-done(((bf16[1,64,1024]{2,1,0:T(8,128)(2,1)}), bf16[16,64,1024]{2,1,0:T(8,128)(2,1)}) %all-gather.2.cloned.1.call-update) | async-done | bytes 2097168 | tf_op jit(solution)/shard_map/all_gather | solution.py:14
  46.6 0.0 copy-start
  46.6 14.8 %conditional.2 = (bf16[1,16,64,4096]{3,2,1,0:T(8,128)(2,1)}) conditional(s32[]{:T(128)} %convert_element_type.23, () %tuple.22, (pred[16,1,1]{0,2,1:T(4,128)(4,1)S(1)}, bf16[16,64,1024]{2,1,0:T(8,128)(2,1)}, bf16[1024,4096]{1,0:T(8,128)(2,1)}) %tuple.36), branch_computations={%region_0.0_spmd, %region_1.2_spmd} | conditional | flops 8598323200 | bytes 18874392 | solution.py:30
  46.6 14.8 %fusion = bf16[1,16,64,4096]{3,2,1,0:T(8,128)(2,1)} fusion(pred[16]{0:T(512)(128)(4,1)S(1)} %bitcast.36, bf16[16,64,1024]{2,1,0:T(8,128)(2,1)} %get-tuple-element.20, bf16[1024,4096]{1,0:T(8,128)(2,1)} %get-tuple-element.21), kind=kOutput, calls=%fused_computation.1 | convolution fusion | flops 8598323200 | bytes 18874384 | tf_op jit(solution)/shard_map/cond/branch_1_fun/dot_general | solution.py:19
  61.4 55.5 %reduce-scatter.2.cloned.1.call-done = f32[1,64,1024]{2,1,0:T(8,128)} async-done(((f32[16,64,1024]{2,1,0:T(8,128)}), f32[1,64,1024]{2,1,0:T(8,128)}) %reduce-scatter.2.cloned.1.call-update) | async-done | bytes 262160 | tf_op jit(solution)/shard_map/reduce_scatter | solution.py:48
  117.0 0.0 copy-done
  117.0 5.8 %fusion.17 = bf16[1,64,4096]{2,1,0:T(8,128)(2,1)} fusion(bf16[1,1024,4096]{2,1,0:T(8,128)(2,1)} %param.13, f32[1,64,1024]{2,1,0:T(8,128)} %reduce-scatter.2.cloned.1.call-done, s32[1,64,1024]{2,1,0:T(8,128)S(1)} %copy-done), kind=kOutput, calls=%fused_computation.11 | convolution fusion | flops 537329664 | bytes 9437184 | tf_op jit(solution)/shard_map/dot_general | solution.py:55
  (1 shorter events, 0.0 us)
Async XLA Ops:
  7.2 39.5 %all-gather.2.cloned.1.call-start = ((), (), s32[]{:S(2)}) async-start(), calls=%async_computation.1 | async-start | bytes 2228224 | tf_op jit(solution)/shard_map/all_gather | solution.py:14
  8.9 108.0 %reduce-scatter.2.cloned.1.call-start = ((), (), s32[]{:S(2)}) async-start(), calls=%async_computation.2 | async-start | bytes 4456448 | tf_op jit(solution)/shard_map/reduce_scatter | solution.py:48
  46.6 70.3 %copy-start = (s32[1,64,1024]{2,1,0:T(8,128)S(1)}, s32[1,64,1024]{2,1,0:T(8,128)}, u32[]{:S(2)}) copy-start(s32[1,64,1024]{2,1,0:T(8,128)} %param.10) | copy-start | bytes 786436
Sparse Core Ops, SparseCore 0:
  10.2 36.3 all-gather.1
  49.6 67.3 reduce-scatter.1
where the time goes:
time: 130 us
  waiting for transfers between devices  78.1 us (60%)
  matrix products  35.7 us (27%)
  between operations  14 us (11%)
  other arithmetic  1.71 us (1%)
    reduce_scatter x1, waiting for transfers between devices, body(): lax.psum_scatter(lax.cond(jnp.int32(0) <= target, code_compute, code_skip...  55.5 us
    all_gather x1, waiting for transfers between devices, body(): gathered = lax.all_gather(active, 'layer', axis=0, tiled=True)  22.5 us
    dot_general x1, matrix products, code_compute(): lax.dot_general(slab_rows.reshape(code_row_count * latents, model_width),...  15.1 us
    dot_general x1, matrix products, decoder_compute(): jnp.dot(gathered.reshape(row_count * latents, tokens), target_error, pref...  14.8 us
    dot_general x1, matrix products, body(): jnp.dot(pre_grad, inputs[0], preferred_element_type=jnp.float32)  5.84 us
  transfers between devices with their start and end apart: 2, of which 2 were waited for; matrix products, arithmetic and copies ran while one was open for 23% of the time, Pallas kernels for 0%

commit v1 on v0

v1 whole, which is shorter than its diff:
```python
import jax
import jax.numpy as jnp
from jax import lax
from jax.sharding import PartitionSpec as P

CORES = 2


def body(saved_codes, relu_mask, errors, decoders, inputs):
    layers = lax.axis_size("layer")
    chips = layers // CORES
    target = lax.axis_index("layer")
    core = target % CORES
    chip = target // CORES
    latents, tokens = saved_codes.shape[1:]
    target_error = errors[0]
    width = target_error.shape[1]
    same_core = [[chip_ * CORES + c for chip_ in range(chips)] for c in range(CORES)]
    swap = [(i, i ^ 1) for i in range(layers)]
    chip_ids = jnp.arange(chips, dtype=jnp.int32)

    active = saved_codes * relu_mask.astype(jnp.bfloat16)
    copies = jnp.broadcast_to(active, (chips, latents, tokens))
    mine = lax.all_to_all(copies, "layer", 0, 0, tiled=True, axis_index_groups=same_core)

    slabs = decoders[0].reshape(chips, CORES, latents, width)
    allowed_mine = chip_ids <= chip
    allowed_other = (chip_ids * CORES + (1 - core)) <= target

    def terms(c, allowed):
        rows = lax.dynamic_index_in_dim(slabs, c, 1, keepdims=False).reshape(chips * latents, width)
        products = lax.dot_general(
            rows, target_error, (((1,), (1,)), ((), ())), preferred_element_type=jnp.float32
        ).reshape(chips, latents, tokens)
        return jnp.where(allowed[:, None, None], products, 0.0)

    away = lax.ppermute(terms(1 - core, allowed_other), "layer", swap)
    pair = (terms(core, allowed_mine) + away).astype(jnp.bfloat16)
    back = lax.all_to_all(pair, "layer", 0, 0, tiled=True, axis_index_groups=same_core)

    other = lax.ppermute(mine, "layer", swap)

    def grads(rows, allowed):
        products = jnp.dot(
            rows.reshape(chips * latents, tokens), target_error, preferred_element_type=jnp.float32
        ).reshape(chips, latents, width)
        return jnp.where(allowed[:, None, None], products, 0.0).astype(jnp.bfloat16)

    own_grads = grads(mine, allowed_mine)
    other_grads = grads(other, allowed_other)
    even = core == 0
    decoder_grad = jnp.stack(
        [jnp.where(even, own_grads, other_grads), jnp.where(even, other_grads, own_grads)], axis=1
    ).reshape(1, layers, latents, width)

    code_grad = jnp.sum(back.astype(jnp.float32), axis=0)
    pre_grad = (code_grad * relu_mask[0].astype(jnp.float32)).astype(jnp.bfloat16)
    encoder_grad = jnp.dot(pre_grad, inputs[0], preferred_element_type=jnp.float32)
    return decoder_grad, code_grad[None], encoder_grad.astype(jnp.bfloat16)[None]


def solution(mesh):
    return jax.shard_map(
        body,
        mesh=mesh,
        in_specs=(
            P("layer", "lat", None),
            P("layer", "lat", None),
            P("layer", None, None),
            P("layer", None, "lat", None),
            P("layer", None, None),
        ),
        out_specs=(P("layer", None, "lat", None), P("layer", "lat", None), P("layer", "lat", None)),
        check_vma=False,
    )
```

time: 130 us -> 92.5 us (0.71); the launches traced: 130 us -> 90.7 us
  waiting for transfers between devices: 78.1 us -> 16.4 us
  between operations: 14 us -> 0.72 us
  matrix products: 35.7 us -> 47.5 us
  starting transfers between devices: 0.08 us -> 9.51 us
  local copies, waits for them, and re-layouts: 0.01 us -> 9 us
  other arithmetic: 1.71 us -> 7.69 us
    reduce_scatter x1 -> x0, waiting for transfers between devices: 55.5 us -> none  [body(): lax.psum_scatter(lax.cond(jnp.int32(0) <= target, code_compute, code_skip...]
    all_gather x1 -> x0, waiting for transfers between devices: 22.5 us -> none  [body(): gathered = lax.all_gather(active, 'layer', axis=0, tiled=True)]
    all_to_all x0 -> x2, waiting for transfers between devices: none -> 16.4 us  [the longest x1 16.4 us: body(): lax.all_to_all(copies, 'layer', 0, 0, tiled=True, axis_index_groups=same_...]
    dot_general x2 -> x4, matrix products: 29.9 us -> 41.6 us  [the longest x2 21.3 us: terms(): lax.dot_general(rows, target_error, (((1,), (1,)), ((), ())), preferred_e...]
    all_to_all x0 -> x2, starting transfers between devices: none -> 9.5 us  [the longest x1 5.77 us: body(): lax.all_to_all(copies, 'layer', 0, 0, tiled=True, axis_index_groups=same_...]
    another operation x0 -> x1, local copies, waits for them, and re-layouts: none -> 7.89 us  [body(): jnp.stack([jnp.where(even, own_grads, other_grads), jnp.where(even, other...]
    another operation x0 -> x1, other arithmetic: none -> 7.47 us  [body(): jnp.stack([jnp.where(even, own_grads, other_grads), jnp.where(even, other...]
    mul x1 -> x0, other arithmetic: 1.7 us -> none  [body(): active = saved_codes * relu_mask.astype(jnp.bfloat16)]
  transfers between devices with their start and end apart: 2 -> 4, of which waited for: 2 -> 1; matrix products, arithmetic and copies ran while one was open for 23% -> 52% of each run, Pallas kernels for 0% -> 0%
where the time goes in v1:
time: 92.5 us; the launch traced here: 90.7 us
  matrix products  47.5 us (51%)
  waiting for transfers between devices  16.4 us (18%)
  starting transfers between devices  9.51 us (10%)
  local copies, waits for them, and re-layouts  9 us (10%)
  other arithmetic  7.69 us (8%)
    dot_general x2, matrix products, terms(): lax.dot_general(rows, target_error, (((1,), (1,)), ((), ())), preferred_e...  21.3 us
    dot_general x2, matrix products, grads(): jnp.dot(rows.reshape(chips * latents, tokens), target_error, preferred_el...  20.3 us
    all_to_all x1, waiting for transfers between devices, body(): lax.all_to_all(copies, 'layer', 0, 0, tiled=True, axis_index_groups=same_...  16.4 us
    another operation x1, local copies, waits for them, and re-layouts, body(): jnp.stack([jnp.where(even, own_grads, other_grads), jnp.where(even, other...  7.89 us
    another operation x1, other arithmetic, body(): jnp.stack([jnp.where(even, own_grads, other_grads), jnp.where(even, other...  7.47 us
    dot_general x1, matrix products, body(): jnp.dot(pre_grad, inputs[0], preferred_element_type=jnp.float32)  5.85 us
    all_to_all x1, starting transfers between devices, body(): lax.all_to_all(copies, 'layer', 0, 0, tiled=True, axis_index_groups=same_...  5.77 us
    all_to_all x1, starting transfers between devices, body(): lax.all_to_all(pair, 'layer', 0, 0, tiled=True, axis_index_groups=same_core)  3.74 us
  transfers between devices with their start and end apart: 4, of which 1 were waited for; matrix products, arithmetic and copies ran while one was open for 52% of the time, Pallas kernels for 0%

profile of v1, /device:TPU:0, one launch (start us, length us, event | category | flops | bytes accessed | tf_op | source)
XLA Modules:
  0.0 90.7 jit_solution(16168360831330589697)
XLA Ops:
  0.7 0.0 copy-start.1
  0.7 0.0 copy-start.2
  0.7 10.5 %fusion.28 = f32[8,64,1024]{2,1,0:T(8,128)} fusion(bf16[1,1024,4096]{2,1,0:T(8,128)(2,1)} %param.7, bf16[8,2,64,4096]{3,2,1,0:T(8,128)(2,1)} %bitcast.60, s32[]{:T(128)S(6)} %select_n.53, pred[8]{0:T(512)(128)(4,1)S(1)} %add_compare_fusion), kind=kOutput, calls=%fused_computation.23 | convolution fusion | flops 4295491584 | bytes 14680076 | tf_op jit(solution)/shard_map/dot_general | solution.py:32
  11.2 0.0 collective-permute-start.1
  11.2 0.0 copy-done.1
  11.2 0.0 copy-done.2
  11.3 1.1 %broadcast_in_dim.55 = bf16[8,64,1024]{2,1,0:T(8,128)(2,1)} broadcast(bf16[64,1024]{1,0:T(8,128)(2,1)S(1)} %multiply_bitcast_fusion), dimensions={1,2} | broadcast | bytes 1179648 | tf_op jit(solution)/shard_map/broadcast_in_dim | solution.py:23
  12.4 5.8 %all-to-all-start = ((bf16[8,64,1024]{2,1,0:T(8,128)(2,1)}), bf16[8,64,1024]{2,1,0:T(8,128)(2,1)S(1)}, u32[]{:S(2)}, u32[]{:S(2)}) async-start(bf16[8,64,1024]{2,1,0:T(8,128)(2,1)} %broadcast_in_dim.55), calls=%async_computation | async-start | bytes 2097152 | tf_op jit(solution)/shard_map/all_to_all | solution.py:24
  18.1 16.4 %all-to-all-done = bf16[8,64,1024]{2,1,0:T(8,128)(2,1)S(1)} async-done(((bf16[8,64,1024]{2,1,0:T(8,128)(2,1)}), bf16[8,64,1024]{2,1,0:T(8,128)(2,1)S(1)}, u32[]{:S(2)}, u32[]{:S(2)}) %all-to-all-start) | async-done | bytes 1048608 | tf_op jit(solution)/shard_map/all_to_all | solution.py:24
  34.5 0.0 collective-permute-start
  34.5 9.4 %select_convert_fusion.1 = bf16[8,64,4096]{2,1,0:T(8,128)(2,1)} fusion(bf16[8,64,1024]{2,1,0:T(8,128)(2,1)S(1)} %all-to-all-done, bf16[1,1024,4096]{2,1,0:T(8,128)(2,1)} %param.7, pred[8]{0:T(512)(128)(4,1)S(1)} %iota_compare_fusion), kind=kOutput, calls=%fused_computation.12 | convolution fusion | flops 4299161600 | bytes 13631496 | tf_op jit(solution)/shard_map/dot_general | solution.py:44
  43.9 0.0 collective-permute-done.1
  43.9 10.8 %add_convert_fusion = bf16[8,64,1024]{2,1,0:T(8,128)(2,1)} fusion(f32[8,64,1024]{2,1,0:T(8,128)} %collective-permute-done.1, bf16[1,1024,4096]{2,1,0:T(8,128)(2,1)} %param.7, bf16[8,2,64,4096]{3,2,1,0:T(8,128)(2,1)} %bitcast.61, s32[]{:T(128)S(6)} %select_n.51, pred[8]{0:T(512)(128)(4,1)S(1)} %iota_compare_fusion), kind=kOutput, calls=%fused_computation.22 | convolution fusion | flops 4296540160 | bytes 15728652 | tf_op jit(solution)/shard_map/dot_general | solution.py:32
  54.7 3.7 %all-to-all-start.1 = ((bf16[8,64,1024]{2,1,0:T(8,128)(2,1)}), bf16[8,64,1024]{2,1,0:T(8,128)(2,1)S(1)}, u32[]{:S(2)}, u32[]{:S(2)}) async-start(bf16[8,64,1024]{2,1,0:T(8,128)(2,1)} %add_convert_fusion), calls=%async_computation.1 | async-start | bytes 2097152 | tf_op jit(solution)/shard_map/all_to_all | solution.py:39
  58.5 0.0 collective-permute-done
  58.5 10.9 %select_bitcast_fusion.1 = (bf16[8,1,64,4096]{3,2,0,1:T(8,128)(2,1)}, bf16[8,1,64,4096]{3,2,0,1:T(8,128)(2,1)}) fusion(bf16[8,64,4096]{2,1,0:T(8,128)(2,1)} %select_convert_fusion.1, pred[]{:T(512)S(6)} %eq.5, bf16[8,64,1024]{2,1,0:T(8,128)(2,1)S(1)} %collective-permute-done, bf16[1,1024,4096]{2,1,0:T(8,128)(2,1)} %param.7, pred[8]{0:T(512)(128)(4,1)S(1)} %add_compare_fusion), kind=kOutput, calls=%fused_computation.20 | convolution fusion | flops 4303355904 | bytes 22020104 | tf_op jit(solution)/shard_map/dot_general | solution.py:44
  69.3 7.5 %pad_maximum_fusion = bf16[8,2,64,4096]{3,2,0,1:T(8,128)(2,1)} fusion(bf16[8,1,64,4096]{3,2,0,1:T(8,128)(2,1)} %get-tuple-element.4, bf16[8,1,64,4096]{3,2,0,1:T(8,128)(2,1)} %get-tuple-element.3), kind=kLoop, calls=%fused_computation | loop fusion | flops 4194304 | bytes 16777216 | tf_op jit(solution)/shard_map/stack | solution.py:52
  76.8 7.9 %copy.10 = bf16[8,2,64,4096]{3,2,1,0:T(8,128)(2,1)} copy(bf16[8,2,64,4096]{3,2,0,1:T(8,128)(2,1)} %pad_maximum_fusion) | data formatting | bytes 16777216 | tf_op jit(solution)/shard_map/stack | solution.py:52
  84.7 0.0 all-to-all-done.1
  84.7 0.2 convert_reduce_fusion
  84.9 0.0 copy-start
  84.9 5.9 %fusion.17 = bf16[1,64,4096]{2,1,0:T(8,128)(2,1)} fusion(bf16[1,1024,4096]{2,1,0:T(8,128)(2,1)} %param.9, f32[1,64,1024]{2,1,0:T(8,128)S(1)} %bitcast.58, s32[1,64,1024]{2,1,0:T(8,128)S(1)} %copy-done.1), kind=kOutput, calls=%fused_computation.14 | convolution fusion | flops 537329664 | bytes 9437184 | tf_op jit(solution)/shard_map/dot_general | solution.py:58
  90.7 0.0 copy-done
  (3 shorter events, 0.0 us)
Async XLA Ops:
  0.7 10.6 %copy-start.1 = (s32[1,64,1024]{2,1,0:T(8,128)S(1)}, s32[1,64,1024]{2,1,0:T(8,128)}, u32[]{:S(2)}) copy-start(s32[1,64,1024]{2,1,0:T(8,128)} %param.6) | copy-start | bytes 786436
  0.7 10.6 %copy-start.2 = (bf16[1,64,1024]{2,1,0:T(8,128)(2,1)S(1)}, bf16[1,64,1024]{2,1,0:T(8,128)(2,1)}, u32[]{:S(2)}) copy-start(bf16[1,64,1024]{2,1,0:T(8,128)(2,1)} %param.5) | copy-start | bytes 393220
  11.2 32.7 %collective-permute-start.1 = (f32[8,64,1024]{2,1,0:T(8,128)}, f32[8,64,1024]{2,1,0:T(8,128)}, u32[]{:S(2)}, u32[]{:S(2)}) collective-permute-start(f32[8,64,1024]{2,1,0:T(8,128)} %fusion.28), channel_id=1, source_target_pairs={{0,8},{8,0},{16,24},{24,16},{32,40},{40,32},{48,56},{56,48},{64,72... | collective-permute-start | bytes 6291464 | tf_op jit(solution)/shard_map/ppermute | solution.py:37
  12.4 22.1 %all-to-all-start = ((bf16[8,64,1024]{2,1,0:T(8,128)(2,1)}), bf16[8,64,1024]{2,1,0:T(8,128)(2,1)S(1)}, u32[]{:S(2)}, u32[]{:S(2)}) async-start(bf16[8,64,1024]{2,1,0:T(8,128)(2,1)} %broadcast_in_dim.55), calls=%async_computation | async-start | bytes 2097152 | tf_op jit(solution)/shard_map/all_to_all | solution.py:24
  34.5 24.0 %collective-permute-start = (bf16[8,64,1024]{2,1,0:T(8,128)(2,1)S(1)}, bf16[8,64,1024]{2,1,0:T(8,128)(2,1)S(1)}, u32[]{:S(2)}, u32[]{:S(2)}) collective-permute-start(bf16[8,64,1024]{2,1,0:T(8,128)(2,1)S(1)} %all-to-all-done), channel_id=1, source_target_pairs={{0,8},{8,0},{16,24},{24,16},{32,40},{40,32},{48,56},{56,48},{64,72... | collective-permute-start | bytes 3145736 | tf_op jit(solution)/shard_map/ppermute | solution.py:41
  54.7 30.0 %all-to-all-start.1 = ((bf16[8,64,1024]{2,1,0:T(8,128)(2,1)}), bf16[8,64,1024]{2,1,0:T(8,128)(2,1)S(1)}, u32[]{:S(2)}, u32[]{:S(2)}) async-start(bf16[8,64,1024]{2,1,0:T(8,128)(2,1)} %add_convert_fusion), calls=%async_computation.1 | async-start | bytes 2097152 | tf_op jit(solution)/shard_map/all_to_all | solution.py:39
  84.9 5.9 %copy-start = (f32[64,1024]{1,0:T(8,128)}, f32[64,1024]{1,0:T(8,128)S(1)}, u32[]{:S(2)}) copy-start(f32[64,1024]{1,0:T(8,128)S(1)} %convert_reduce_fusion) | copy-start | bytes 786436

commit v2 on v1

v2 whole, which is shorter than its diff:
```python
import jax
import jax.numpy as jnp
from jax import lax
from jax.experimental import pallas as pl
from jax.experimental.pallas import tpu as pltpu
from jax.sharding import PartitionSpec as P


CORES = 2
AHEAD = 3
DEPTHS = (256, 512, 1024, 1024, 1280)
COLUMNS = (512, 1024, 1024, 768, 512, 256)

HBM = pl.BlockSpec(memory_space=pltpu.HBM)
VMEM = pl.BlockSpec(memory_space=pltpu.VMEM)
SMEM = pl.BlockSpec(memory_space=pltpu.SMEM)


def params(mib):
    return pltpu.CompilerParams(vmem_limit_bytes=mib << 20)


def starts(sizes):
    return [sum(sizes[:i]) for i in range(len(sizes))]


def gate(codes, mask, chips):
    latents, tokens = codes.shape

    def kernel(codes_hbm, mask_hbm, out_hbm, buf, mask_buf, sems):
        loads = [
            pltpu.make_async_copy(codes_hbm, buf, sems.at[chips]),
            pltpu.make_async_copy(mask_hbm, mask_buf, sems.at[chips + 1]),
        ]
        copies = [
            pltpu.make_async_copy(buf, out_hbm.at[chip], sems.at[chip]) for chip in range(chips)
        ]
        for load in loads:
            load.start()
        for load in loads:
            load.wait()
        buf[...] = buf[...] * mask_buf[...].astype(jnp.bfloat16)
        for copy in copies:
            copy.start()
        for copy in copies:
            copy.wait()

    return pl.pallas_call(
        kernel,
        out_shape=jax.ShapeDtypeStruct((chips, latents, tokens), jnp.bfloat16),
        in_specs=[HBM, HBM],
        out_specs=HBM,
        scratch_shapes=[
            pltpu.VMEM((latents, tokens), jnp.bfloat16),
            pltpu.VMEM((latents, tokens), jnp.int32),
            pltpu.SemaphoreType.DMA((chips + 2,)),
        ],
        compiler_params=params(4),
        name="gate",
    )(codes, mask)


def code_terms(place, slabs, errors, hand_on):
    chips, _, latents, width = slabs.shape
    tokens = errors.shape[0]
    rows = chips * latents
    offsets = starts(DEPTHS)
    steps = len(DEPTHS)
    parts = 2

    def kernel(place_ref, slab_hbm, error_hbm, out, *refs):
        acc = refs[0] if hand_on else out
        slab_buf, error_buf, sems, out_sems = refs[-4:]
        parity, target = place_ref[0], place_ref[1]
        loads = []
        for k in range(steps):
            cols = pl.ds(offsets[k], DEPTHS[k])
            loads.append((
                pltpu.make_async_copy(error_hbm.at[:, cols], error_buf.at[:, cols], sems.at[0, k]),
                pltpu.make_async_copy(
                    slab_hbm.at[:, parity, :, cols], slab_buf.at[:, :, cols], sems.at[1, k]
                ),
            ))
        for pair in loads[:AHEAD]:
            for load in pair:
                load.start()
        source = (lax.broadcasted_iota(jnp.int32, (1, rows), 1) // latents) * CORES + parity
        keep = (source <= target).astype(jnp.float32)
        stores = []
        for k in range(steps):
            cols = pl.ds(offsets[k], DEPTHS[k])
            for load in loads[k]:
                load.wait()
            if k + AHEAD < steps:
                for load in loads[k + AHEAD]:
                    load.start()
            last = k == steps - 1
            count = parts if last else 1
            wide = rows // count
            for n in range(count):
                here = pl.ds(n * wide, wide)
                some = pl.ds(n * (chips // count), chips // count)
                part = lax.dot_general(
                    error_buf[:, cols], slab_buf[some, :, cols].reshape(wide, DEPTHS[k]),
                    (((1,), (1,)), ((), ())), preferred_element_type=jnp.float32,
                )
                if k == 0:
                    acc[:, here] = part
                elif not last:
                    acc[:, here] += part
                else:
                    acc[:, here] = (acc[:, here] + part) * keep[:, n * wide : (n + 1) * wide]
                    if hand_on:
                        store = pltpu.make_async_copy(
                            acc.at[:, here], out.at[:, here], out_sems.at[n]
                        )
                        store.start()
                        stores.append(store)
        for store in stores:
            store.wait()

    scratch = [
        pltpu.VMEM((chips, latents, width), jnp.bfloat16),
        pltpu.VMEM((tokens, width), jnp.bfloat16),
        pltpu.SemaphoreType.DMA((2, steps)),
        pltpu.SemaphoreType.DMA((parts,)),
    ]
    if hand_on:
        scratch = [pltpu.VMEM((tokens, rows), jnp.float32)] + scratch
    return pl.pallas_call(
        kernel,
        out_shape=jax.ShapeDtypeStruct((tokens, rows), jnp.float32),
        in_specs=[SMEM, HBM, HBM],
        out_specs=HBM if hand_on else VMEM,
        scratch_shapes=scratch,
        compiler_params=params(24),
        cost_estimate=pl.CostEstimate(
            flops=2 * rows * tokens * width, transcendentals=0,
            bytes_accessed=2 * (rows + tokens) * width,
        ),
        name="code_away" if hand_on else "code_own",
    )(place, slabs, errors)


def join(own, away, chips):
    tokens, rows = own.shape
    latents = rows // chips
    half, lanes = tokens // 2, CORES * latents
    pairs = rows // lanes

    def kernel(own_ref, away_ref, out_hbm, out_buf, sems):
        left = lax.broadcasted_iota(jnp.int32, (half, lanes), 1) < latents
        stores = []
        for pair in range(pairs):
            cols = pl.ds(pair * lanes, lanes)
            low = own_ref[pl.ds(0, half), cols] + away_ref[pl.ds(0, half), cols]
            high = own_ref[pl.ds(half, half), cols] + away_ref[pl.ds(half, half), cols]
            out_buf[2 * pair] = jnp.where(
                left, low, pltpu.roll(high, latents, axis=1)
            ).astype(jnp.bfloat16)
            out_buf[2 * pair + 1] = jnp.where(
                left, pltpu.roll(low, latents, axis=1), high
            ).astype(jnp.bfloat16)
            both = pl.ds(2 * pair, 2)
            store = pltpu.make_async_copy(out_buf.at[both], out_hbm.at[both], sems.at[pair])
            store.start()
            stores.append(store)
        for store in stores:
            store.wait()

    return pl.pallas_call(
        kernel,
        out_shape=jax.ShapeDtypeStruct((chips, half, lanes), jnp.bfloat16),
        in_specs=[VMEM, VMEM],
        out_specs=HBM,
        scratch_shapes=[
            pltpu.VMEM((chips, half, lanes), jnp.bfloat16),
            pltpu.SemaphoreType.DMA((pairs,)),
        ],
        compiler_params=params(8),
        name="join",
    )(own, away)


def decoder(place, own, other, errors):
    tokens, width = errors.shape
    chips, latents, _ = own.shape
    rows = chips * CORES * latents
    offsets = starts(COLUMNS)
    steps = len(COLUMNS)

    def kernel(place_ref, error_hbm, own_ref, other_ref, out_hbm, lhs, error_buf, out_buf, sems):
        parity, target = place_ref[0], place_ref[1]
        loads, stores = [], []
        for k in range(steps):
            cols = pl.ds(offsets[k], COLUMNS[k])
            loads.append(
                pltpu.make_async_copy(error_hbm.at[:, cols], error_buf.at[:, cols], sems.at[0, k])
            )
            stores.append(
                pltpu.make_async_copy(out_buf.at[:, cols], out_hbm.at[:, cols], sems.at[1, k])
            )
        for load in loads[:AHEAD]:
            load.start()
        for ref, side in ((own_ref, parity), (other_ref, 1 - parity)):
            for chip in range(chips):
                source = chip * CORES + side
                value = ref[chip]
                there = pl.ds(pl.multiple_of(source * latents, latents), latents)
                lhs[there, :] = jnp.where(source <= target, value, jnp.zeros_like(value))
        for k in range(steps):
            cols = pl.ds(offsets[k], COLUMNS[k])
            loads[k].wait()
            if k + AHEAD < steps:
                loads[k + AHEAD].start()
            out_buf[:, cols] = jnp.dot(
                lhs[...], error_buf[:, cols], preferred_element_type=jnp.float32
            ).astype(jnp.bfloat16)
            stores[k].start()
        for store in stores:
            store.wait()

    return pl.pallas_call(
        kernel,
        out_shape=jax.ShapeDtypeStruct((rows, width), jnp.bfloat16),
        in_specs=[SMEM, HBM, VMEM, VMEM],
        out_specs=HBM,
        scratch_shapes=[
            pltpu.VMEM((rows, tokens), jnp.bfloat16),
            pltpu.VMEM((tokens, width), jnp.bfloat16),
            pltpu.VMEM((rows, width), jnp.bfloat16),
            pltpu.SemaphoreType.DMA((2, steps)),
        ],
        compiler_params=params(28),
        cost_estimate=pl.CostEstimate(
            flops=2 * rows * tokens * width, transcendentals=0,
            bytes_accessed=2 * (rows + tokens) * width,
        ),
        name="decoder",
    )(place, errors, own, other)


def encoder(parts, mask, inputs):
    tokens, width = inputs.shape
    chips = parts.shape[0]
    latents = mask.shape[0]
    columns = 1024
    steps = width // columns

    def kernel(parts_ref, mask_ref, input_hbm, code_ref, out_ref, buf, sems):
        loads = []
        for k in range(steps):
            cols = pl.ds(k * columns, columns)
            loads.append(pltpu.make_async_copy(input_hbm.at[:, cols], buf.at[k], sems.at[k]))
        for load in loads[:AHEAD]:
            load.start()
        total = parts_ref[0].astype(jnp.float32)
        for chip in range(1, chips):
            total = total + parts_ref[chip].astype(jnp.float32)
        total = total.T
        code = jnp.concatenate([total[:latents], total[latents:]], axis=1)
        code_ref[...] = code
        pre = (code * mask_ref[...].astype(jnp.float32)).astype(jnp.bfloat16)
        for k in range(steps):
            loads[k].wait()
            if k + AHEAD < steps:
                loads[k + AHEAD].start()
            out_ref[:, pl.ds(k * columns, columns)] = jnp.dot(
                pre, buf[k], preferred_element_type=jnp.float32
            ).astype(jnp.bfloat16)

    return pl.pallas_call(
        kernel,
        out_shape=[
            jax.ShapeDtypeStruct((latents, tokens), jnp.float32),
            jax.ShapeDtypeStruct((latents, width), jnp.bfloat16),
        ],
        in_specs=[VMEM, VMEM, HBM],
        out_specs=[VMEM, VMEM],
        scratch_shapes=[
            pltpu.VMEM((steps, tokens, columns), jnp.bfloat16),
            pltpu.SemaphoreType.DMA((steps,)),
        ],
        compiler_params=params(16),
        name="encoder",
    )(parts, mask, inputs)


def step(saved_codes, relu_mask, errors, decoders, inputs):
    layers = lax.axis_size("layer")
    chips = layers // CORES
    target = lax.axis_index("layer")
    core = target % CORES
    latents, _ = saved_codes.shape[1:]
    hbm = lambda value: pltpu.with_memory_space_constraint(value, pltpu.HBM)
    target_error = hbm(errors[0])
    width = target_error.shape[1]
    swap = [(i, i ^ 1) for i in range(layers)]
    same_core = [[chip * CORES + c for chip in range(chips)] for c in range(CORES)]
    place_own = jnp.stack([core, target]).astype(jnp.int32)
    place_other = jnp.stack([1 - core, target]).astype(jnp.int32)

    def exchange(value):
        return lax.all_to_all(value, "layer", 0, 0, tiled=True, axis_index_groups=same_core)

    slabs = hbm(decoders[0].reshape(chips, CORES, latents, width))
    copies = gate(hbm(saved_codes[0]), hbm(relu_mask[0]), chips)
    mine = exchange(copies)
    away = code_terms(place_other, slabs, target_error, True)
    away = lax.ppermute(away, "layer", swap)
    own = code_terms(place_own, slabs, target_error, False)
    own, away = lax.optimization_barrier((own, away))
    terms = join(own, away, chips)
    terms, mine = lax.optimization_barrier((terms, mine))
    other = lax.ppermute(mine, "layer", swap)
    parts = exchange(terms)
    grads = decoder(place_own, mine, other, target_error)

    parts, grads = lax.optimization_barrier((parts, grads))
    code_grad, encoder_grad = encoder(parts, relu_mask[0], hbm(inputs[0]))
    return grads.reshape(1, layers, latents, width), code_grad[None], encoder_grad[None]


def solution(mesh):
    return jax.shard_map(
        step,
        mesh=mesh,
        in_specs=(
            P("layer", "lat", None),
            P("layer", "lat", None),
            P("layer", None, None),
            P("layer", None, "lat", None),
            P("layer", None, None),
        ),
        out_specs=(P("layer", None, "lat", None), P("layer", "lat", None), P("layer", "lat", None)),
        check_vma=False,
    )
```

time: 92.5 us -> 60 us (0.65)
  matrix products: 47.5 us -> 0 us
  Pallas kernels: 0 us -> 38.7 us
  local copies, waits for them, and re-layouts: 9 us -> 0.01 us
  other arithmetic: 7.69 us -> 0.15 us
  waiting for transfers between devices: 16.4 us -> 9.76 us
    dot_general x5 -> x0, matrix products: 47.5 us -> none  [the longest x2 21.3 us: terms(): lax.dot_general(rows, target_error, (((1,), (1,)), ((), ())), preferred_e...]
    pallas_call x0 -> x6, Pallas kernels: none -> 38.7 us  [the longest x2 15.8 us: code_terms(): pl.pallas_call(kernel, out_shape=jax.ShapeDtypeStruct((tokens, rows), jnp...]
    another operation x1 -> x0, local copies, waits for them, and re-layouts: 7.89 us -> none  [body(): jnp.stack([jnp.where(even, own_grads, other_grads), jnp.where(even, other...]
    another operation x1 -> x2, other arithmetic: 7.47 us -> 0.15 us  [the longest x1 0.08 us: step(): place_other = jnp.stack([1 - core, target]).astype(jnp.int32)]
    all_to_all x2, waiting for transfers between devices: 16.4 us -> 9.76 us  [exchange(): lax.all_to_all(value, 'layer', 0, 0, tiled=True, axis_index_groups=same_c...]
    broadcast_in_dim x1 -> x0, local copies, waits for them, and re-layouts: 1.1 us -> none  [body(): copies = jnp.broadcast_to(active, (chips, latents, tokens))]
  transfers between devices with their start and end apart: 4 -> 4, of which waited for: 1 -> 2; matrix products, arithmetic and copies ran while one was open for 52% -> 0% of each run, Pallas kernels for 0% -> 42%
where the time goes in v2:
time: 60 us; the launch traced here: 59.1 us
  Pallas kernels  38.7 us (65%)
  waiting for transfers between devices  9.76 us (16%)
  starting transfers between devices  9.61 us (16%)
  between operations  0.89 us (1%)
    pallas_call x2, Pallas kernels, code_terms(): pl.pallas_call(kernel, out_shape=jax.ShapeDtypeStruct((tokens, rows), jnp...  15.8 us
    pallas_call x1, Pallas kernels, decoder(): pl.pallas_call(kernel, out_shape=jax.ShapeDtypeStruct((rows, width), jnp....  14.3 us
    all_to_all x2, waiting for transfers between devices, exchange(): lax.all_to_all(value, 'layer', 0, 0, tiled=True, axis_index_groups=same_c...  9.76 us
    all_to_all x2, starting transfers between devices, exchange(): lax.all_to_all(value, 'layer', 0, 0, tiled=True, axis_index_groups=same_c...  9.52 us
    pallas_call x1, Pallas kernels, encoder(): pl.pallas_call(kernel, out_shape=[jax.ShapeDtypeStruct((latents, tokens),...  5.09 us
    pallas_call x1, Pallas kernels, gate(): pl.pallas_call(kernel, out_shape=jax.ShapeDtypeStruct((chips, latents, to...  2.16 us
    pallas_call x1, Pallas kernels, join(): pl.pallas_call(kernel, out_shape=jax.ShapeDtypeStruct((chips, half, lanes...  1.41 us
  transfers between devices with their start and end apart: 4, of which 2 were waited for; matrix products, arithmetic and copies ran while one was open for 0% of the time, Pallas kernels for 42%

profile of v2, /device:TPU:0, one launch (start us, length us, event | category | flops | bytes accessed | tf_op | source)
XLA Modules:
  0.0 59.1 jit_solution(1508011277576101646)
XLA Ops:
  0.6 0.1 pad_add_fusion.1.place_ref
  0.7 8.6 %code_away.1 = f32[1024,512]{1,0:T(8,128)} custom-call(s32[2]{0:T(128)S(1)} %pad_add_fusion.1.place_ref, bf16[8,2,64,4096]{3,2,1,0:T(8,128)(2,1)} %bitcast.13, bf16[1024,4096]{1,0:T(8,128)(2,1)} %bitcast.15), custom_call_target="tpu_custom_call" | custom-call | flops 4294967296 | bytes 12582912 | tf_op jit(solution)/shard_map/code_away/pallas_call | solution.py:130
  9.3 0.1 collective-permute-start
  9.4 2.2 %gate.1 = bf16[8,64,1024]{2,1,0:T(8,128)(2,1)} custom-call(bf16[64,1024]{1,0:T(8,128)(2,1)} %bitcast.19, s32[64,1024]{1,0:T(8,128)} %bitcast.11), custom_call_target="tpu_custom_call" | custom-call | tf_op jit(solution)/shard_map/gate/pallas_call | solution.py:48
  11.6 5.8 %all-to-all-start = ((bf16[8,64,1024]{2,1,0:T(8,128)(2,1)}), bf16[8,64,1024]{2,1,0:T(8,128)(2,1)S(1)}, u32[]{:S(2)}, u32[]{:S(2)}) async-start(bf16[8,64,1024]{2,1,0:T(8,128)(2,1)} %gate.1), calls=%async_computation | async-start | bytes 2097152 | tf_op jit(solution)/shard_map/all_to_all | solution.py:304
  17.4 0.1 pad_add_fusion.place_ref
  17.4 7.2 %code_own.1.own_ref = f32[1024,512]{1,0:T(8,128)S(1)} custom-call(s32[2]{0:T(128)S(1)} %pad_add_fusion.place_ref, bf16[8,2,64,4096]{3,2,1,0:T(8,128)(2,1)} %bitcast.14, bf16[1024,4096]{1,0:T(8,128)(2,1)} %bitcast.16), custom_call_target="tpu_custom_call" | custom-call | flops 4294967296 | bytes 12582912 | tf_op jit(solution)/shard_map/code_own/pallas_call | solution.py:130
  24.6 0.0 collective-permute-done.away_ref
  24.6 1.4 %join.1 = bf16[8,512,128]{2,1,0:T(8,128)(2,1)} custom-call(f32[1024,512]{1,0:T(8,128)S(1)} %code_own.1.own_ref, f32[1024,512]{1,0:T(8,128)S(1)} %collective-permute-done.away_ref), custom_call_target="tpu_custom_call" | custom-call | tf_op jit(solution)/shard_map/join/pallas_call | solution.py:171
  26.0 7.7 %all-to-all-done.own_ref = bf16[8,64,1024]{2,1,0:T(8,128)(2,1)S(1)} async-done(((bf16[8,64,1024]{2,1,0:T(8,128)(2,1)}), bf16[8,64,1024]{2,1,0:T(8,128)(2,1)S(1)}, u32[]{:S(2)}, u32[]{:S(2)}) %all-to-all-start) | async-done | bytes 1048608 | tf_op jit(solution)/shard_map/all_to_all | solution.py:304
  33.7 0.0 collective-permute-start.1
  33.7 3.7 %all-to-all-start.1 = ((bf16[8,512,128]{2,1,0:T(8,128)(2,1)}), bf16[8,512,128]{2,1,0:T(8,128)(2,1)S(1)}, u32[]{:S(2)}, u32[]{:S(2)}) async-start(bf16[8,512,128]{2,1,0:T(8,128)(2,1)} %join.1), calls=%async_computation.1 | async-start | bytes 2097152 | tf_op jit(solution)/shard_map/all_to_all | solution.py:304
  37.5 0.0 copy-start
  37.5 0.0 collective-permute-done.1.other_ref
  37.5 14.3 %decoder.1 = bf16[1024,4096]{1,0:T(8,128)(2,1)} custom-call(s32[2]{0:T(128)S(1)} %pad_add_fusion.place_ref, bf16[1024,4096]{1,0:T(8,128)(2,1)} %bitcast.17, bf16[8,64,1024]{2,1,0:T(8,128)(2,1)S(1)} %all-to-all-done.own_ref, bf16[8,64,1024]{2,1,0:T(8,128)(2,1)} %collective-permute-done.1.other_ref), custom_call_target="tpu_custom_call" | custom-call | flops 8589934592 | bytes 16777216 | tf_op jit(solution)/shard_map/decoder/pallas_call | solution.py:223
  51.8 2.1 %all-to-all-done.1.parts_ref = bf16[8,512,128]{2,1,0:T(8,128)(2,1)S(1)} async-done(((bf16[8,512,128]{2,1,0:T(8,128)(2,1)}), bf16[8,512,128]{2,1,0:T(8,128)(2,1)S(1)}, u32[]{:S(2)}, u32[]{:S(2)}) %all-to-all-start.1) | async-done | bytes 1048608 | tf_op jit(solution)/shard_map/all_to_all | solution.py:304
  53.9 0.0 copy-done
  53.9 5.1 %encoder.1 = (f32[64,1024]{1,0:T(8,128)}, bf16[64,4096]{1,0:T(8,128)(2,1)}) custom-call(bf16[8,512,128]{2,1,0:T(8,128)(2,1)S(1)} %all-to-all-done.1.parts_ref, s32[64,1024]{1,0:T(8,128)S(1)} %bitcast.12, bf16[1024,4096]{1,0:T(8,128)(2,1)} %bitcast.18), custom_call_target="tpu_custom_call" | custom-call | tf_op jit(solution)/shard_map/encoder/pallas_call | solution.py:272
Async XLA Ops:
  9.3 15.3 %collective-permute-start = (f32[1024,512]{1,0:T(8,128)}, f32[1024,512]{1,0:T(8,128)S(1)}, u32[]{:S(2)}, u32[]{:S(2)}) collective-permute-start(f32[1024,512]{1,0:T(8,128)} %code_away.1), channel_id=1, source_target_pairs={{0,8},{8,0},{16,24},{24,16},{32,40},{40,32},{48,56},{56,48},{64,72... | collective-permute-start | bytes 6291464 | tf_op jit(solution)/shard_map/ppermute | solution.py:310
  11.6 22.1 %all-to-all-start = ((bf16[8,64,1024]{2,1,0:T(8,128)(2,1)}), bf16[8,64,1024]{2,1,0:T(8,128)(2,1)S(1)}, u32[]{:S(2)}, u32[]{:S(2)}) async-start(bf16[8,64,1024]{2,1,0:T(8,128)(2,1)} %gate.1), calls=%async_computation | async-start | bytes 2097152 | tf_op jit(solution)/shard_map/all_to_all | solution.py:304
  33.7 3.8 %collective-permute-start.1 = (bf16[8,64,1024]{2,1,0:T(8,128)(2,1)S(1)}, bf16[8,64,1024]{2,1,0:T(8,128)(2,1)}, u32[]{:S(2)}, u32[]{:S(2)}) collective-permute-start(bf16[8,64,1024]{2,1,0:T(8,128)(2,1)S(1)} %all-to-all-done.own_ref), channel_id=1, source_target_pairs={{0,8},{8,0},{16,24},{24,16},{32,40},{40,32},{48,56},{56,48},{64,72... | collective-permute-start | bytes 3145736 | tf_op jit(solution)/shard_map/ppermute | solution.py:315
  33.7 20.2 %all-to-all-start.1 = ((bf16[8,512,128]{2,1,0:T(8,128)(2,1)}), bf16[8,512,128]{2,1,0:T(8,128)(2,1)S(1)}, u32[]{:S(2)}, u32[]{:S(2)}) async-start(bf16[8,512,128]{2,1,0:T(8,128)(2,1)} %join.1), calls=%async_computation.1 | async-start | bytes 2097152 | tf_op jit(solution)/shard_map/all_to_all | solution.py:304
  37.5 16.4 %copy-start = (s32[1,64,1024]{2,1,0:T(8,128)S(1)}, s32[1,64,1024]{2,1,0:T(8,128)}, u32[]{:S(2)}) copy-start(s32[1,64,1024]{2,1,0:T(8,128)} %param.6) | copy-start | bytes 786436

commit v3 on v2

v3 whole, which is shorter than its diff:
```python
import jax
import jax.numpy as jnp
from jax import lax
from jax.experimental import pallas as pl
from jax.experimental.pallas import tpu as pltpu
from jax.sharding import PartitionSpec as P


CORES = 2
AHEAD = 2
HELD = 1024
DEPTHS = (HELD, 1024, 1024, 1024)
COLUMNS = (512, 1536, 1536, 512)
FIRST = 512
REST = (1024, 1280, 1280)

HBM = pl.BlockSpec(memory_space=pltpu.HBM)
VMEM = pl.BlockSpec(memory_space=pltpu.VMEM)
SMEM = pl.BlockSpec(memory_space=pltpu.SMEM)


def params(mib):
    return pltpu.CompilerParams(vmem_limit_bytes=mib << 20)


def starts(sizes):
    return [sum(sizes[:i]) for i in range(len(sizes))]


def gate(place, slabs, errors, codes, mask):
    latents, tokens = codes.shape
    chips = slabs.shape[0]

    def kernel(
        place_ref, slab_hbm, error_hbm, codes_hbm, mask_hbm, out_hbm, error_ref, slab_ref,
        buf, mask_buf, sems,
    ):
        cols = pl.ds(0, HELD)
        loads = [
            pltpu.make_async_copy(codes_hbm, buf, sems.at[chips]),
            pltpu.make_async_copy(mask_hbm, mask_buf, sems.at[chips + 1]),
        ]
        held = [
            pltpu.make_async_copy(
                slab_hbm.at[:, place_ref[0], :, cols], slab_ref, sems.at[chips + 2]
            ),
            pltpu.make_async_copy(error_hbm.at[:, cols], error_ref, sems.at[chips + 3]),
        ]
        copies = [
            pltpu.make_async_copy(buf, out_hbm.at[chip], sems.at[chip]) for chip in range(chips)
        ]
        for load in loads + held:
            load.start()
        for load in loads:
            load.wait()
        buf[...] = buf[...] * mask_buf[...].astype(jnp.bfloat16)
        for copy in copies:
            copy.start()
        for copy in copies + held:
            copy.wait()

    return pl.pallas_call(
        kernel,
        out_shape=[
            pltpu.HBM((chips, latents, tokens), jnp.bfloat16),
            jax.ShapeDtypeStruct((tokens, HELD), jnp.bfloat16),
            jax.ShapeDtypeStruct((chips, latents, HELD), jnp.bfloat16),
        ],
        in_specs=[SMEM, HBM, HBM, HBM, HBM],
        out_specs=[HBM, VMEM, VMEM],
        scratch_shapes=[
            pltpu.VMEM((latents, tokens), jnp.bfloat16),
            pltpu.VMEM((latents, tokens), jnp.int32),
            pltpu.SemaphoreType.DMA((chips + 4,)),
        ],
        compiler_params=params(8),
        name="gate",
    )(place, slabs, errors, codes, mask)


def code_terms(place, slabs, errors, *held, inputs=None):
    chips, _, latents, width = slabs.shape
    tokens = errors.shape[0]
    rows = chips * latents
    offsets = starts(DEPTHS)
    steps = len(DEPTHS)

    def kernel(place_ref, slab_hbm, error_hbm, *refs):
        held_refs = refs[: len(held)]
        slab_buf, error_buf, sems = refs[-3:]
        out = refs[-4]
        if inputs is not None:
            input_hbm, first_ref, out = refs[len(held) : len(held) + 3]
            first = pltpu.make_async_copy(
                input_hbm.at[:, pl.ds(0, FIRST)], first_ref, sems.at[0, 0]
            )
        parity, target = place_ref[0], place_ref[1]
        loads = []
        for k in range(steps):
            cols = pl.ds(offsets[k], DEPTHS[k])
            group = []
            if k or not held:
                group.append(
                    pltpu.make_async_copy(
                        error_hbm.at[:, cols], error_buf.at[:, cols], sems.at[0, k]
                    )
                )
            if k or len(held) < 2:
                group.append(
                    pltpu.make_async_copy(
                        slab_hbm.at[:, parity, :, cols], slab_buf.at[:, :, cols], sems.at[1, k]
                    )
                )
            loads.append(group)
        for pair in loads[:AHEAD]:
            for load in pair:
                load.start()
        source = (lax.broadcasted_iota(jnp.int32, (1, rows), 1) // latents) * CORES + parity
        keep = (source <= target).astype(jnp.float32)
        for k in range(steps):
            cols = pl.ds(offsets[k], DEPTHS[k])
            for load in loads[k]:
                load.wait()
            if k + AHEAD < steps:
                for load in loads[k + AHEAD]:
                    load.start()
            error = held_refs[0][...] if k == 0 and held else error_buf[:, cols]
            slab = held_refs[1][...] if k == 0 and len(held) > 1 else slab_buf[:, :, cols]
            part = lax.dot_general(
                error, slab.reshape(rows, DEPTHS[k]),
                (((1,), (1,)), ((), ())), preferred_element_type=jnp.float32,
            )
            if k == 0:
                out[...] = part
            elif k < steps - 1:
                out[...] += part
            else:
                out[...] = (out[...] + part) * keep
            if inputs is not None and k == steps - 1 - AHEAD:
                first.start()
        if inputs is not None:
            first.wait()

    out_shape = [jax.ShapeDtypeStruct((tokens, rows), jnp.float32)]
    extra = ()
    if inputs is not None:
        out_shape = [jax.ShapeDtypeStruct((tokens, FIRST), jnp.bfloat16)] + out_shape
        extra = (inputs,)
    return pl.pallas_call(
        kernel,
        out_shape=out_shape,
        in_specs=[SMEM, HBM, HBM] + [VMEM] * len(held) + [HBM] * len(extra),
        out_specs=[VMEM] * len(out_shape),
        scratch_shapes=[
            pltpu.VMEM((chips, latents, width), jnp.bfloat16),
            pltpu.VMEM((tokens, width), jnp.bfloat16),
            pltpu.SemaphoreType.DMA((2, steps)),
        ],
        compiler_params=params(24),
        cost_estimate=pl.CostEstimate(
            flops=2 * rows * tokens * width, transcendentals=0,
            bytes_accessed=2 * (rows + tokens) * width,
        ),
    )(place, slabs, errors, *held, *extra)


def join(own, away, chips):
    tokens, rows = own.shape
    latents = rows // chips
    half, lanes = tokens // 2, CORES * latents
    pairs = rows // lanes

    def kernel(own_ref, away_ref, out_hbm, out_buf, sems):
        left = lax.broadcasted_iota(jnp.int32, (half, lanes), 1) < latents
        stores = []
        for pair in range(pairs):
            cols = pl.ds(pair * lanes, lanes)
            low = own_ref[pl.ds(0, half), cols] + away_ref[pl.ds(0, half), cols]
            high = own_ref[pl.ds(half, half), cols] + away_ref[pl.ds(half, half), cols]
            out_buf[2 * pair] = jnp.where(
                left, low, pltpu.roll(high, latents, axis=1)
            ).astype(jnp.bfloat16)
            out_buf[2 * pair + 1] = jnp.where(
                left, pltpu.roll(low, latents, axis=1), high
            ).astype(jnp.bfloat16)
            both = pl.ds(2 * pair, 2)
            store = pltpu.make_async_copy(out_buf.at[both], out_hbm.at[both], sems.at[pair])
            store.start()
            stores.append(store)
        for store in stores:
            store.wait()

    return pl.pallas_call(
        kernel,
        out_shape=jax.ShapeDtypeStruct((chips, half, lanes), jnp.bfloat16),
        in_specs=[VMEM, VMEM],
        out_specs=HBM,
        scratch_shapes=[
            pltpu.VMEM((chips, half, lanes), jnp.bfloat16),
            pltpu.SemaphoreType.DMA((pairs,)),
        ],
        compiler_params=params(8),
        name="join",
    )(own, away)


def decoder(place, own, other, errors):
    tokens, width = errors.shape
    chips, latents, _ = own.shape
    rows = chips * CORES * latents
    offsets = starts(COLUMNS)
    steps = len(COLUMNS)

    def kernel(
        place_ref, error_hbm, own_ref, other_ref, out_hbm, lhs, error_buf, out_buf, sems
    ):
        parity, target = place_ref[0], place_ref[1]
        loads, stores = [], []
        for k in range(steps):
            cols = pl.ds(offsets[k], COLUMNS[k])
            loads.append(
                pltpu.make_async_copy(error_hbm.at[:, cols], error_buf.at[:, cols], sems.at[0, k])
            )
            stores.append(
                pltpu.make_async_copy(out_buf.at[:, cols], out_hbm.at[:, cols], sems.at[1, k])
            )
        rows_in = [
            pltpu.make_async_copy(ref, lhs.at[:, side], sems.at[2, 1 + n])
            for n, (ref, side) in enumerate(((own_ref, parity), (other_ref, 1 - parity)))
        ]
        for copy in rows_in:
            copy.start()
        for load in loads[:AHEAD]:
            load.start()
        for copy in rows_in:
            copy.wait()
        for source in range(chips * CORES):
            @pl.when(source > target)
            def _(source=source):
                lhs[source // CORES, source % CORES] = jnp.zeros((latents, tokens), jnp.bfloat16)

        for k in range(steps):
            cols = pl.ds(offsets[k], COLUMNS[k])
            loads[k].wait()
            if k + AHEAD < steps:
                loads[k + AHEAD].start()
            out_buf[:, cols] = jnp.dot(
                lhs[...].reshape(rows, tokens), error_buf[:, cols], preferred_element_type=jnp.float32
            ).astype(jnp.bfloat16)
            stores[k].start()
        for store in stores:
            store.wait()

    return pl.pallas_call(
        kernel,
        out_shape=jax.ShapeDtypeStruct((rows, width), jnp.bfloat16),
        in_specs=[SMEM, HBM, HBM, HBM],
        out_specs=HBM,
        scratch_shapes=[
            pltpu.VMEM((chips, CORES, latents, tokens), jnp.bfloat16),
            pltpu.VMEM((tokens, width), jnp.bfloat16),
            pltpu.VMEM((rows, width), jnp.bfloat16),
            pltpu.SemaphoreType.DMA((3, steps)),
        ],
        compiler_params=params(28),
        cost_estimate=pl.CostEstimate(
            flops=2 * rows * tokens * width, transcendentals=0,
            bytes_accessed=2 * (rows + tokens) * width,
        ),
        name="decoder",
    )(place, errors, own, other)


def encoder(parts, mask, inputs, held):
    tokens, width = inputs.shape
    chips = parts.shape[0]
    latents = mask.shape[0]
    sizes = (FIRST, *REST)
    offsets = starts(sizes)
    steps = len(sizes)

    def kernel(
        parts_ref, mask_ref, input_hbm, held_ref, code_hbm, out_hbm, buf, code_buf, out_buf, sems
    ):
        loads, stores = [None], []
        for k in range(steps):
            cols = pl.ds(offsets[k], sizes[k])
            if k:
                loads.append(
                    pltpu.make_async_copy(input_hbm.at[:, cols], buf.at[:, cols], sems.at[0, k])
                )
                loads[k].start()
            stores.append(
                pltpu.make_async_copy(out_buf.at[:, cols], out_hbm.at[:, cols], sems.at[1, k])
            )
        total = parts_ref[0].astype(jnp.float32)
        for chip in range(1, chips):
            total = total + parts_ref[chip].astype(jnp.float32)
        total = total.T
        code = jnp.concatenate([total[:latents], total[latents:]], axis=1)
        code_buf[...] = code
        stores.append(pltpu.make_async_copy(code_buf, code_hbm, sems.at[0, 0]))
        stores[-1].start()
        pre = (code * mask_ref[...].astype(jnp.float32)).astype(jnp.bfloat16)
        for k in range(steps):
            cols = pl.ds(offsets[k], sizes[k])
            if k:
                loads[k].wait()
            out_buf[:, cols] = jnp.dot(
                pre, buf[:, cols] if k else held_ref[...], preferred_element_type=jnp.float32
            ).astype(jnp.bfloat16)
            stores[k].start()
        for store in stores:
            store.wait()

    return pl.pallas_call(
        kernel,
        out_shape=[
            pltpu.HBM((latents, tokens), jnp.float32),
            pltpu.HBM((latents, width), jnp.bfloat16),
        ],
        in_specs=[VMEM, VMEM, HBM, VMEM],
        out_specs=[HBM, HBM],
        scratch_shapes=[
            pltpu.VMEM((tokens, width), jnp.bfloat16),
            pltpu.VMEM((latents, tokens), jnp.float32),
            pltpu.VMEM((latents, width), jnp.bfloat16),
            pltpu.SemaphoreType.DMA((2, steps)),
        ],
        compiler_params=params(16),
        name="encoder",
    )(parts, mask, inputs, held)


def step(saved_codes, relu_mask, errors, decoders, inputs):
    layers = lax.axis_size("layer")
    chips = layers // CORES
    target = lax.axis_index("layer")
    core = target % CORES
    latents, _ = saved_codes.shape[1:]
    hbm = lambda value: pltpu.with_memory_space_constraint(value, pltpu.HBM)
    target_error, layer_inputs = hbm(errors[0]), hbm(inputs[0])
    width = target_error.shape[1]
    swap = [(i, i ^ 1) for i in range(layers)]
    same_core = [[chip * CORES + c for chip in range(chips)] for c in range(CORES)]
    place_own = jnp.stack([core, target]).astype(jnp.int32)
    place_other = jnp.stack([1 - core, target]).astype(jnp.int32)

    def exchange(value):
        return lax.all_to_all(value, "layer", 0, 0, tiled=True, axis_index_groups=same_core)

    slabs = hbm(decoders[0].reshape(chips, CORES, latents, width))
    copies, held_error, held_slab = gate(
        place_other, slabs, target_error, hbm(saved_codes[0]), hbm(relu_mask[0])
    )
    mine = exchange(copies)
    (away,) = code_terms(place_other, slabs, target_error, held_error, held_slab)
    away = lax.ppermute(away, "layer", swap)
    held_inputs, own = code_terms(place_own, slabs, target_error, held_error, inputs=layer_inputs)
    own, away = lax.optimization_barrier((own, away))
    terms = join(own, away, chips)
    terms, mine = lax.optimization_barrier((terms, mine))
    other = lax.ppermute(mine, "layer", swap)
    parts = exchange(terms)
    grads = decoder(place_own, hbm(mine), hbm(other), target_error)

    parts, grads = lax.optimization_barrier((parts, grads))
    code_grad, encoder_grad = encoder(
        parts, relu_mask[0], layer_inputs, held_inputs
    )
    return grads.reshape(1, layers, latents, width), code_grad[None], encoder_grad[None]


def solution(mesh):
    return jax.shard_map(
        step,
        mesh=mesh,
        in_specs=(
            P("layer", "lat", None),
            P("layer", "lat", None),
            P("layer", None, None),
            P("layer", None, "lat", None),
            P("layer", None, None),
        ),
        out_specs=(P("layer", None, "lat", None), P("layer", "lat", None), P("layer", "lat", None)),
        check_vma=False,
    )
```

time: 60 us -> 59.5 us (level)
  Pallas kernels: 38.7 us -> 37.7 us
  waiting for transfers between devices: 9.76 us -> 10.5 us
    pallas_call x1, Pallas kernels: 1.41 us -> 2.99 us  [join(): pl.pallas_call(kernel, out_shape=jax.ShapeDtypeStruct((chips, half, lanes...]
    pallas_call x1, Pallas kernels: 14.3 us -> 12.8 us  [decoder(): pl.pallas_call(kernel, out_shape=jax.ShapeDtypeStruct((rows, width), jnp....]
    pallas_call x4, Pallas kernels: 23 us -> 21.9 us  [the longest x2 14.1 us: code_terms(): pl.pallas_call(kernel, out_shape=out_shape, in_specs=[SMEM, HBM, HBM] + [...]
    all_to_all x2, waiting for transfers between devices: 9.76 us -> 10.5 us  [exchange(): lax.all_to_all(value, 'layer', 0, 0, tiled=True, axis_index_groups=same_c...]
  transfers between devices with their start and end apart: 4 -> 4, of which waited for: 2 -> 2; matrix products, arithmetic and copies ran while one was open for 0% -> 0% of each run, Pallas kernels for 42% -> 38%
where the time goes in v3:
time: 59.5 us; the launch traced here: 58.6 us
  Pallas kernels  37.7 us (63%)
  waiting for transfers between devices  10.5 us (18%)
  starting transfers between devices  9.41 us (16%)
  between operations  0.88 us (1%)
    pallas_call x2, Pallas kernels, code_terms(): pl.pallas_call(kernel, out_shape=out_shape, in_specs=[SMEM, HBM, HBM] + [...  14.1 us
    pallas_call x1, Pallas kernels, decoder(): pl.pallas_call(kernel, out_shape=jax.ShapeDtypeStruct((rows, width), jnp....  12.8 us
    all_to_all x2, waiting for transfers between devices, exchange(): lax.all_to_all(value, 'layer', 0, 0, tiled=True, axis_index_groups=same_c...  10.5 us
    all_to_all x2, starting transfers between devices, exchange(): lax.all_to_all(value, 'layer', 0, 0, tiled=True, axis_index_groups=same_c...  9.33 us
    pallas_call x1, Pallas kernels, encoder(): pl.pallas_call(kernel, out_shape=[pltpu.HBM((latents, tokens), jnp.float3...  4.98 us
    pallas_call x1, Pallas kernels, join(): pl.pallas_call(kernel, out_shape=jax.ShapeDtypeStruct((chips, half, lanes...  2.99 us
    pallas_call x1, Pallas kernels, gate(): pl.pallas_call(kernel, out_shape=[pltpu.HBM((chips, latents, tokens), jnp...  2.84 us
  transfers between devices with their start and end apart: 4, of which 2 were waited for; matrix products, arithmetic and copies ran while one was open for 0% of the time, Pallas kernels for 38%

profile of v3, /device:TPU:0, one launch (start us, length us, event | category | flops | bytes accessed | tf_op | source)
XLA Modules:
  0.0 58.6 jit_solution(4353340608989691834)
XLA Ops:
  0.6 0.1 pad_add_fusion
  0.7 2.8 %gate.1 = (bf16[8,64,1024]{2,1,0:T(8,128)(2,1)}, bf16[1024,1024]{1,0:T(8,128)(2,1)S(1)}, bf16[8,64,1024]{2,1,0:T(8,128)(2,1)S(1)}) custom-call(s32[2]{0:T(128)S(1)} %get-tuple-element.30.place_ref, bf16[8,2,64,4096]{3,2,1,0:T(8,128)(2,1)} %bitcast.13, bf16[1024,4096]{1,0:T(8,128)(2,1)} %bitcast.16, bf16[64,1024]{1,0:T(8,128)(2,1)} %bitcast.22, ...), custom_call_target="tpu_custom_call" | custom-call | tf_op jit(solution)/shard_map/gate/pallas_call | solution.py:62
  3.6 7.4 %shard_map.77 = f32[1024,512]{1,0:T(8,128)} custom-call(s32[2]{0:T(128)S(1)} %get-tuple-element.30.place_ref, bf16[8,2,64,4096]{3,2,1,0:T(8,128)(2,1)} %bitcast.14, bf16[1024,4096]{1,0:T(8,128)(2,1)} %bitcast.17, bf16[1024,1024]{1,0:T(8,128)(2,1)S(1)} %get-tuple-element.16.refs_0_, bf16[8,64,1024]{2,1,0:T(8,128)(2,1)S(1)} %get-tuple-element.18.refs_1_), custom_call_target="tpu_custom_call" | custom-call | flops 4294967296 | bytes 12582912 | tf_op jit(solution)/shard_map/pallas_call | solution.py:149
  11.0 0.1 collective-permute-start
  11.1 5.8 %all-to-all-start = ((bf16[8,64,1024]{2,1,0:T(8,128)(2,1)}), bf16[8,64,1024]{2,1,0:T(8,128)(2,1)}, u32[]{:S(2)}, u32[]{:S(2)}) async-start(bf16[8,64,1024]{2,1,0:T(8,128)(2,1)} %get-tuple-element.21), calls=%async_computation | async-start | bytes 2097152 | tf_op jit(solution)/shard_map/all_to_all | solution.py:350
  16.9 6.6 %shard_map.76 = (bf16[1024,512]{1,0:T(8,128)(2,1)S(1)}, f32[1024,512]{1,0:T(8,128)S(1)}) custom-call(s32[2]{0:T(128)S(1)} %get-tuple-element.29.place_ref, bf16[8,2,64,4096]{3,2,1,0:T(8,128)(2,1)} %bitcast.15, bf16[1024,4096]{1,0:T(8,128)(2,1)} %bitcast.18, bf16[1024,1024]{1,0:T(8,128)(2,1)S(1)} %get-tuple-element.16.refs_0_, bf16[1024,4096]{1,0:T(8,128)(2,1)} %bitcast.20), custom_call_target="tpu_custom_call" | custom-call | flops 4294967296 | bytes 12582912 | tf_op jit(solution)/shard_map/pallas_call | solution.py:149
  23.5 0.0 collective-permute-done.away_ref
  23.5 3.0 %join.1 = bf16[8,512,128]{2,1,0:T(8,128)(2,1)} custom-call(f32[1024,512]{1,0:T(8,128)S(1)} %get-tuple-element.19.own_ref, f32[1024,512]{1,0:T(8,128)} %collective-permute-done.away_ref), custom_call_target="tpu_custom_call" | custom-call | tf_op jit(solution)/shard_map/join/pallas_call | solution.py:193
  26.5 6.8 %all-to-all-done.own_ref = bf16[8,64,1024]{2,1,0:T(8,128)(2,1)} async-done(((bf16[8,64,1024]{2,1,0:T(8,128)(2,1)}), bf16[8,64,1024]{2,1,0:T(8,128)(2,1)}, u32[]{:S(2)}, u32[]{:S(2)}) %all-to-all-start) | async-done | bytes 1048608 | tf_op jit(solution)/shard_map/all_to_all | solution.py:350
  33.3 0.0 collective-permute-start.1
  33.3 3.6 %all-to-all-start.1 = ((bf16[8,512,128]{2,1,0:T(8,128)(2,1)}), bf16[8,512,128]{2,1,0:T(8,128)(2,1)S(1)}, u32[]{:S(2)}, u32[]{:S(2)}) async-start(bf16[8,512,128]{2,1,0:T(8,128)(2,1)} %join.1), calls=%async_computation.1 | async-start | bytes 2097152 | tf_op jit(solution)/shard_map/all_to_all | solution.py:350
  36.9 0.0 copy-start
  36.9 0.0 collective-permute-done.1.other_ref
  36.9 12.8 %decoder.1 = bf16[1024,4096]{1,0:T(8,128)(2,1)} custom-call(s32[2]{0:T(128)S(1)} %get-tuple-element.29.place_ref, bf16[1024,4096]{1,0:T(8,128)(2,1)} %bitcast.19, bf16[8,64,1024]{2,1,0:T(8,128)(2,1)} %all-to-all-done.own_ref, bf16[8,64,1024]{2,1,0:T(8,128)(2,1)} %collective-permute-done.1.other_ref), custom_call_target="tpu_custom_call" | custom-call | flops 8589934592 | bytes 16777216 | tf_op jit(solution)/shard_map/decoder/pallas_call | solution.py:254
  49.7 3.7 %all-to-all-done.1.parts_ref = bf16[8,512,128]{2,1,0:T(8,128)(2,1)S(1)} async-done(((bf16[8,512,128]{2,1,0:T(8,128)(2,1)}), bf16[8,512,128]{2,1,0:T(8,128)(2,1)S(1)}, u32[]{:S(2)}, u32[]{:S(2)}) %all-to-all-start.1) | async-done | bytes 1048608 | tf_op jit(solution)/shard_map/all_to_all | solution.py:350
  53.5 0.0 copy-done
  53.5 5.0 %encoder.1 = (f32[64,1024]{1,0:T(8,128)}, bf16[64,4096]{1,0:T(8,128)(2,1)}) custom-call(bf16[8,512,128]{2,1,0:T(8,128)(2,1)S(1)} %all-to-all-done.1.parts_ref, s32[64,1024]{1,0:T(8,128)S(1)} %bitcast.12, bf16[1024,4096]{1,0:T(8,128)(2,1)} %bitcast.21, bf16[1024,512]{1,0:T(8,128)(2,1)S(1)} %get-tuple-element.26.held_ref), custom_call_target="tpu_custom_call" | custom-call | tf_op jit(solution)/shard_map/encoder/pallas_call | solution.py:316
Async XLA Ops:
  11.0 12.5 %collective-permute-start = (f32[1024,512]{1,0:T(8,128)}, f32[1024,512]{1,0:T(8,128)}, u32[]{:S(2)}, u32[]{:S(2)}) collective-permute-start(f32[1024,512]{1,0:T(8,128)} %shard_map.77), channel_id=1, source_target_pairs={{0,8},{8,0},{16,24},{24,16},{32,40},{40,32},{48,56},{56,48},{64,72... | collective-permute-start | bytes 6291464 | tf_op jit(solution)/shard_map/ppermute | solution.py:358
  11.1 22.2 %all-to-all-start = ((bf16[8,64,1024]{2,1,0:T(8,128)(2,1)}), bf16[8,64,1024]{2,1,0:T(8,128)(2,1)}, u32[]{:S(2)}, u32[]{:S(2)}) async-start(bf16[8,64,1024]{2,1,0:T(8,128)(2,1)} %get-tuple-element.21), calls=%async_computation | async-start | bytes 2097152 | tf_op jit(solution)/shard_map/all_to_all | solution.py:350
  33.3 3.6 %collective-permute-start.1 = (bf16[8,64,1024]{2,1,0:T(8,128)(2,1)}, bf16[8,64,1024]{2,1,0:T(8,128)(2,1)}, u32[]{:S(2)}, u32[]{:S(2)}) collective-permute-start(bf16[8,64,1024]{2,1,0:T(8,128)(2,1)} %all-to-all-done.own_ref), channel_id=1, source_target_pairs={{0,8},{8,0},{16,24},{24,16},{32,40},{40,32},{48,56},{56,48},{64,72... | collective-permute-start | bytes 3145736 | tf_op jit(solution)/shard_map/ppermute | solution.py:363
  33.3 20.2 %all-to-all-start.1 = ((bf16[8,512,128]{2,1,0:T(8,128)(2,1)}), bf16[8,512,128]{2,1,0:T(8,128)(2,1)S(1)}, u32[]{:S(2)}, u32[]{:S(2)}) async-start(bf16[8,512,128]{2,1,0:T(8,128)(2,1)} %join.1), calls=%async_computation.1 | async-start | bytes 2097152 | tf_op jit(solution)/shard_map/all_to_all | solution.py:350
  36.9 16.6 %copy-start = (s32[1,64,1024]{2,1,0:T(8,128)S(1)}, s32[1,64,1024]{2,1,0:T(8,128)}, u32[]{:S(2)}) copy-start(s32[1,64,1024]{2,1,0:T(8,128)} %param.6) | copy-start | bytes 786436

commit v4 on v3

--- a/solution.py
+++ b/solution.py
@@ -12,7 +12,7 @@
 DEPTHS = (HELD, 1024, 1024, 1024)
 COLUMNS = (512, 1536, 1536, 512)
 FIRST = 512
-REST = (1024, 1280, 1280)
+REST = (512,) * 7
 
 HBM = pl.BlockSpec(memory_space=pltpu.HBM)
 VMEM = pl.BlockSpec(memory_space=pltpu.VMEM)
@@ -88,11 +88,15 @@
     def kernel(place_ref, slab_hbm, error_hbm, *refs):
         held_refs = refs[: len(held)]
         slab_buf, error_buf, sems = refs[-3:]
-        out = refs[-4]
         if inputs is not None:
             input_hbm, first_ref, out = refs[len(held) : len(held) + 3]
             first = pltpu.make_async_copy(
                 input_hbm.at[:, pl.ds(0, FIRST)], first_ref, sems.at[0, 0]
+            )
+        else:
+            first_ref, out = refs[len(held) : len(held) + 2]
+            first = pltpu.make_async_copy(
+                slab_hbm.at[:, 1 - place_ref[0], :, pl.ds(0, HELD)], first_ref, sems.at[0, 0]
             )
         parity, target = place_ref[0], place_ref[1]
         loads = []
@@ -136,16 +140,17 @@
                 out[...] += part
             else:
                 out[...] = (out[...] + part) * keep
-            if inputs is not None and k == steps - 1 - AHEAD:
+            if k == steps - 1 - AHEAD:
                 first.start()
-        if inputs is not None:
-            first.wait()
-
-    out_shape = [jax.ShapeDtypeStruct((tokens, rows), jnp.float32)]
-    extra = ()
-    if inputs is not None:
-        out_shape = [jax.ShapeDtypeStruct((tokens, FIRST), jnp.bfloat16)] + out_shape
-        extra = (inputs,)
+        first.wait()
+
+    out_shape = [
+        jax.ShapeDtypeStruct((chips, latents, HELD), jnp.bfloat16)
+        if inputs is None
+        else jax.ShapeDtypeStruct((tokens, FIRST), jnp.bfloat16),
+        jax.ShapeDtypeStruct((tokens, rows), jnp.float32),
+    ]
+    extra = () if inputs is None else (inputs,)
     return pl.pallas_call(
         kernel,
         out_shape=out_shape,
@@ -354,9 +359,11 @@
         place_other, slabs, target_error, hbm(saved_codes[0]), hbm(relu_mask[0])
     )
     mine = exchange(copies)
-    (away,) = code_terms(place_other, slabs, target_error, held_error, held_slab)
+    next_slab, away = code_terms(place_other, slabs, target_error, held_error, held_slab)
     away = lax.ppermute(away, "layer", swap)
-    held_inputs, own = code_terms(place_own, slabs, target_error, held_error, inputs=layer_inputs)
+    held_inputs, own = code_terms(
+        place_own, slabs, target_error, held_error, next_slab, inputs=layer_inputs
+    )
     own, away = lax.optimization_barrier((own, away))
     terms = join(own, away, chips)
     terms, mine = lax.optimization_barrier((terms, mine))

time: 59.5 us -> 60.1 us (1.010)
  local copies, waits for them, and re-layouts: 0.01 us -> 2.18 us
  Pallas kernels: 37.7 us -> 36.8 us
  waiting for transfers between devices: 10.5 us -> 9.87 us
    unnamed x2 -> x6, local copies, waits for them, and re-layouts: 0.01 us -> 2.18 us
    all_to_all x2, waiting for transfers between devices: 10.5 us -> 9.87 us  [exchange(): lax.all_to_all(value, 'layer', 0, 0, tiled=True, axis_index_groups=same_c...]
  transfers between devices with their start and end apart: 4 -> 4, of which waited for: 2 -> 2; matrix products, arithmetic and copies ran while one was open for 0% -> 0% of each run, Pallas kernels for 38% -> 37%
where the time goes in v4:
time: 60.1 us; the launch traced here: 59.2 us
  Pallas kernels  36.8 us (61%)
  waiting for transfers between devices  9.87 us (16%)
  starting transfers between devices  9.33 us (16%)
  local copies, waits for them, and re-layouts  2.18 us (4%)
  between operations  0.89 us (1%)
    pallas_call x2, Pallas kernels, code_terms(): pl.pallas_call(kernel, out_shape=out_shape, in_specs=[SMEM, HBM, HBM] + [...  13.5 us
    pallas_call x1, Pallas kernels, decoder(): pl.pallas_call(kernel, out_shape=jax.ShapeDtypeStruct((rows, width), jnp....  12.8 us
    all_to_all x2, waiting for transfers between devices, exchange(): lax.all_to_all(value, 'layer', 0, 0, tiled=True, axis_index_groups=same_c...  9.87 us
    all_to_all x2, starting transfers between devices, exchange(): lax.all_to_all(value, 'layer', 0, 0, tiled=True, axis_index_groups=same_c...  9.33 us
    pallas_call x1, Pallas kernels, encoder(): pl.pallas_call(kernel, out_shape=[pltpu.HBM((latents, tokens), jnp.float3...  4.67 us
    pallas_call x1, Pallas kernels, join(): pl.pallas_call(kernel, out_shape=jax.ShapeDtypeStruct((chips, half, lanes...  2.99 us
    pallas_call x1, Pallas kernels, gate(): pl.pallas_call(kernel, out_shape=[pltpu.HBM((chips, latents, tokens), jnp...  2.84 us
    unnamed x6, local copies, waits for them, and re-layouts  2.18 us
  transfers between devices with their start and end apart: 4, of which 2 were waited for; matrix products, arithmetic and copies ran while one was open for 0% of the time, Pallas kernels for 37%

profile of v4, /device:TPU:0, one launch (start us, length us, event | category | flops | bytes accessed | tf_op | source)
XLA Modules:
  0.0 59.2 jit_solution(9762200682672924893)
XLA Ops:
  0.6 0.1 pad_add_fusion
  0.7 2.8 %gate.1 = (bf16[8,64,1024]{2,1,0:T(8,128)(2,1)}, bf16[1024,1024]{1,0:T(8,128)(2,1)S(1)}, bf16[8,64,1024]{2,1,0:T(8,128)(2,1)S(1)}) custom-call(s32[2]{0:T(128)S(1)} %get-tuple-element.34.place_ref, bf16[8,2,64,4096]{3,2,1,0:T(8,128)(2,1)} %bitcast.13, bf16[1024,4096]{1,0:T(8,128)(2,1)} %bitcast.16, bf16[64,1024]{1,0:T(8,128)(2,1)} %bitcast.22, ...), custom_call_target="tpu_custom_call" | custom-call | tf_op jit(solution)/shard_map/gate/pallas_call | solution.py:62
  3.6 7.4 %shard_map.76 = (bf16[8,64,1024]{2,1,0:T(8,128)(2,1)S(1)}, f32[1024,512]{1,0:T(8,128)}) custom-call(s32[2]{0:T(128)S(1)} %get-tuple-element.34.place_ref, bf16[8,2,64,4096]{3,2,1,0:T(8,128)(2,1)} %bitcast.14, bf16[1024,4096]{1,0:T(8,128)(2,1)} %bitcast.17, bf16[1024,1024]{1,0:T(8,128)(2,1)S(1)} %get-tuple-element.18.refs_0_, ...), custom_call_target="tpu_custom_call" | custom-call | flops 4294967296 | bytes 12582912 | tf_op jit(solution)/shard_map/pallas_call | solution.py:154
  11.0 0.0 copy-start.1
  11.0 1.0 %copy-done.1 = bf16[8,64,1024]{2,1,0:T(8,128)(2,1)} copy-done((bf16[8,64,1024]{2,1,0:T(8,128)(2,1)}, bf16[8,64,1024]{2,1,0:T(8,128)(2,1)S(1)}, u32[]{:S(2)}) %copy-start.1) | copy-done | bytes 1048600
  12.0 0.0 collective-permute-start
  12.0 5.8 %all-to-all-start = ((bf16[8,64,1024]{2,1,0:T(8,128)(2,1)}), bf16[8,64,1024]{2,1,0:T(8,128)(2,1)}, u32[]{:S(2)}, u32[]{:S(2)}) async-start(bf16[8,64,1024]{2,1,0:T(8,128)(2,1)} %get-tuple-element.25), calls=%async_computation | async-start | bytes 2097152 | tf_op jit(solution)/shard_map/all_to_all | solution.py:355
  17.7 0.0 copy-start.2
  17.7 1.2 %copy-done.2 = bf16[8,64,1024]{2,1,0:T(8,128)(2,1)S(1)} copy-done((bf16[8,64,1024]{2,1,0:T(8,128)(2,1)S(1)}, bf16[8,64,1024]{2,1,0:T(8,128)(2,1)}, u32[]{:S(2)}) %copy-start.2) | copy-done | bytes 1048600
  19.0 6.1 %shard_map.77 = (bf16[1024,512]{1,0:T(8,128)(2,1)S(1)}, f32[1024,512]{1,0:T(8,128)S(1)}) custom-call(s32[2]{0:T(128)S(1)} %get-tuple-element.33.place_ref, bf16[8,2,64,4096]{3,2,1,0:T(8,128)(2,1)} %bitcast.15, bf16[1024,4096]{1,0:T(8,128)(2,1)} %bitcast.18, bf16[1024,1024]{1,0:T(8,128)(2,1)S(1)} %get-tuple-element.18.refs_0_, ...), custom_call_target="tpu_custom_call" | custom-call | flops 4294967296 | bytes 12582912 | tf_op jit(solution)/shard_map/pallas_call | solution.py:154
  25.1 0.0 collective-permute-done.away_ref
  25.1 3.0 %join.1 = bf16[8,512,128]{2,1,0:T(8,128)(2,1)} custom-call(f32[1024,512]{1,0:T(8,128)S(1)} %get-tuple-element.23.own_ref, f32[1024,512]{1,0:T(8,128)} %collective-permute-done.away_ref), custom_call_target="tpu_custom_call" | custom-call | tf_op jit(solution)/shard_map/join/pallas_call | solution.py:198
  28.1 6.1 %all-to-all-done.own_ref = bf16[8,64,1024]{2,1,0:T(8,128)(2,1)} async-done(((bf16[8,64,1024]{2,1,0:T(8,128)(2,1)}), bf16[8,64,1024]{2,1,0:T(8,128)(2,1)}, u32[]{:S(2)}, u32[]{:S(2)}) %all-to-all-start) | async-done | bytes 1048608 | tf_op jit(solution)/shard_map/all_to_all | solution.py:355
  34.2 0.0 collective-permute-start.1
  34.2 3.6 %all-to-all-start.1 = ((bf16[8,512,128]{2,1,0:T(8,128)(2,1)}), bf16[8,512,128]{2,1,0:T(8,128)(2,1)S(1)}, u32[]{:S(2)}, u32[]{:S(2)}) async-start(bf16[8,512,128]{2,1,0:T(8,128)(2,1)} %join.1), calls=%async_computation.1 | async-start | bytes 2097152 | tf_op jit(solution)/shard_map/all_to_all | solution.py:355
  37.8 0.0 copy-start
  37.8 0.0 collective-permute-done.1.other_ref
  37.8 12.8 %decoder.1 = bf16[1024,4096]{1,0:T(8,128)(2,1)} custom-call(s32[2]{0:T(128)S(1)} %get-tuple-element.33.place_ref, bf16[1024,4096]{1,0:T(8,128)(2,1)} %bitcast.19, bf16[8,64,1024]{2,1,0:T(8,128)(2,1)} %all-to-all-done.own_ref, bf16[8,64,1024]{2,1,0:T(8,128)(2,1)} %collective-permute-done.1.other_ref), custom_call_target="tpu_custom_call" | custom-call | flops 8589934592 | bytes 16777216 | tf_op jit(solution)/shard_map/decoder/pallas_call | solution.py:259
  50.6 3.7 %all-to-all-done.1.parts_ref = bf16[8,512,128]{2,1,0:T(8,128)(2,1)S(1)} async-done(((bf16[8,512,128]{2,1,0:T(8,128)(2,1)}), bf16[8,512,128]{2,1,0:T(8,128)(2,1)S(1)}, u32[]{:S(2)}, u32[]{:S(2)}) %all-to-all-start.1) | async-done | bytes 1048608 | tf_op jit(solution)/shard_map/all_to_all | solution.py:355
  54.4 0.0 copy-done
  54.4 4.7 %encoder.1 = (f32[64,1024]{1,0:T(8,128)}, bf16[64,4096]{1,0:T(8,128)(2,1)}) custom-call(bf16[8,512,128]{2,1,0:T(8,128)(2,1)S(1)} %all-to-all-done.1.parts_ref, s32[64,1024]{1,0:T(8,128)S(1)} %bitcast.12, bf16[1024,4096]{1,0:T(8,128)(2,1)} %bitcast.21, bf16[1024,512]{1,0:T(8,128)(2,1)S(1)} %get-tuple-element.30.held_ref), custom_call_target="tpu_custom_call" | custom-call | tf_op jit(solution)/shard_map/encoder/pallas_call | solution.py:321
Async XLA Ops:
  11.0 1.0 %copy-start.1 = (bf16[8,64,1024]{2,1,0:T(8,128)(2,1)}, bf16[8,64,1024]{2,1,0:T(8,128)(2,1)S(1)}, u32[]{:S(2)}) copy-start(bf16[8,64,1024]{2,1,0:T(8,128)(2,1)S(1)} %get-tuple-element.20.refs_1_) | copy-start | bytes 3145732
  12.0 13.1 %collective-permute-start = (f32[1024,512]{1,0:T(8,128)}, f32[1024,512]{1,0:T(8,128)}, u32[]{:S(2)}, u32[]{:S(2)}) collective-permute-start(f32[1024,512]{1,0:T(8,128)} %get-tuple-element.22), channel_id=1, source_target_pairs={{0,8},{8,0},{16,24},{24,16},{32,40},{40,32},{48,56},{56,48},{64,72... | collective-permute-start | bytes 6291464 | tf_op jit(solution)/shard_map/ppermute | solution.py:363
  12.0 22.2 %all-to-all-start = ((bf16[8,64,1024]{2,1,0:T(8,128)(2,1)}), bf16[8,64,1024]{2,1,0:T(8,128)(2,1)}, u32[]{:S(2)}, u32[]{:S(2)}) async-start(bf16[8,64,1024]{2,1,0:T(8,128)(2,1)} %get-tuple-element.25), calls=%async_computation | async-start | bytes 2097152 | tf_op jit(solution)/shard_map/all_to_all | solution.py:355
  17.7 1.2 %copy-start.2 = (bf16[8,64,1024]{2,1,0:T(8,128)(2,1)S(1)}, bf16[8,64,1024]{2,1,0:T(8,128)(2,1)}, u32[]{:S(2)}) copy-start(bf16[8,64,1024]{2,1,0:T(8,128)(2,1)} %copy-done.1) | copy-start | bytes 3145732
  34.2 3.6 %collective-permute-start.1 = (bf16[8,64,1024]{2,1,0:T(8,128)(2,1)}, bf16[8,64,1024]{2,1,0:T(8,128)(2,1)}, u32[]{:S(2)}, u32[]{:S(2)}) collective-permute-start(bf16[8,64,1024]{2,1,0:T(8,128)(2,1)} %all-to-all-done.own_ref), channel_id=1, source_target_pairs={{0,8},{8,0},{16,24},{24,16},{32,40},{40,32},{48,56},{56,48},{64,72... | collective-permute-start | bytes 3145736 | tf_op jit(solution)/shard_map/ppermute | solution.py:370
  34.2 20.2 %all-to-all-start.1 = ((bf16[8,512,128]{2,1,0:T(8,128)(2,1)}), bf16[8,512,128]{2,1,0:T(8,128)(2,1)S(1)}, u32[]{:S(2)}, u32[]{:S(2)}) async-start(bf16[8,512,128]{2,1,0:T(8,128)(2,1)} %join.1), calls=%async_computation.1 | async-start | bytes 2097152 | tf_op jit(solution)/shard_map/all_to_all | solution.py:355
  37.8 16.6 %copy-start = (s32[1,64,1024]{2,1,0:T(8,128)S(1)}, s32[1,64,1024]{2,1,0:T(8,128)}, u32[]{:S(2)}) copy-start(s32[1,64,1024]{2,1,0:T(8,128)} %param.6) | copy-start | bytes 786436
